TPU v7x, 32 devices: a whole 2x2x4 slice. The times are simulated.
32 devices in a mesh: brick: 8 (over y, x, core), help: 4 (over z).
Axes of the slice: x: 2, y: 2, z: 4, core: 2. Of those that a mesh axis runs over, the one named last changes fastest.
Arguments:
- positions: float32 [3, 2048], P(None, ('brick', 'help')), may hold values from 0 to 1
- velocities: float32 [3, 2048], P(None, ('brick', 'help')), may hold values from -5 to 5
- forces_in: float32 [3, 2048], P(None, ('brick', 'help')), may hold values from -5 to 5
- neighbors: int32 [2048, 128], P(('brick', 'help')), may hold values from -1 to 767, as said below
- w_embed1: float32 [32], replicated, may hold values from -4 to 4
- b_embed1: float32 [32], replicated, may hold values from -3 to 3
- w_embed2: bfloat16 [32, 64], replicated, may hold values from -1 to 1
- b_embed2: float32 [64], replicated, may hold values from -3 to 3
- w_embed3: bfloat16 [64, 128], replicated, may hold values from -0.75 to 0.75
- b_embed3: float32 [128], replicated, may hold values from -3 to 3
- w_fit1: bfloat16 [2048, 240], replicated, may hold values from -0.125 to 0.125
- b_fit1: float32 [240], replicated, may hold values from -3 to 3
- w_fit2: bfloat16 [240, 240], replicated, may hold values from -0.375 to 0.375
- b_fit2: float32 [240], replicated, may hold values from -3 to 3
- w_out: float32 [240], replicated, may hold values from -0.375 to 0.375
Outputs:
- positions_out: float32 [3, 2048], P(None, ('brick', 'help'))
- velocities_out: float32 [3, 2048], P(None, ('brick', 'help'))
- energy: float32 [2048], P(('brick', 'help'))
- forces_out: float32 [3, 2048], P(None, ('brick', 'help'))
Inputs may be any that keep to these rules, and one draw needn't show every extreme that they name: `neighbors`: row i holds atom i's neighbours as table entries: 0 to 255 the atoms of the brick before its own (cyclically), 256 to 511 its own brick, 512 to 767 the brick after; -1 pads. Live entries come first, an entry may repeat, an atom never lists itself. In the first half of the bricks an atom has 96 to 128 live entries, in the other bricks 128 / 4 to 64.
All inputs are finite; a program needn't handle non-finite values.
Results may differ from a plain program's by a relative error of at most 0.011.
Values sent between devices are 32-bit elements; how exact they have to be, the bound alone decides.
No kernel may reach another device: no remote copies, remote signals or barrier semaphores. Data moves between devices by JAX's collectives and lax.ppermute only.
A program may use at most 64 MiB of HBM per device.

v0:
```python
import jax
import jax.numpy as jnp
from jax import lax
from jax.sharding import PartitionSpec as P

NEIGHBOUR_SLOTS = 128
M2 = 16
STEPS = 2
kick_scale = 0.25
time_step = 0.05
highest_precision = lax.Precision.HIGHEST


def extended(value, sides, width):
    for axis, dim in sides:
        size, length = (lax.axis_size(axis), value.shape[dim])
        up = [(i, (i + 1) % size) for i in range(size)]
        down = [(j, i) for i, j in up]
        last = lax.slice_in_dim(value, length - width, length, axis=dim)
        first = lax.slice_in_dim(value, 0, width, axis=dim)
        before = lax.ppermute(last, axis, up)
        after = lax.ppermute(first, axis, down)
        value = jnp.concatenate([before, value, after], axis=dim)
    return value


def pair_terms(displace, live_mask, weights):
    (
        w_embed1,
        b_embed1,
        w_embed2,
        b_embed2,
        w_embed3,
        b_embed3,
        w_fit1,
        b_fit1,
        w_fit2,
        b_fit2,
        w_out,
    ) = weights
    blocks, slot_count = live_mask.shape
    quad_dist = jnp.sum(displace * displace, axis=0) + 0.25
    radius = jnp.sqrt(quad_dist)
    smooth = live_mask / radius
    environment_matrix = jnp.concatenate(
        [smooth[None], live_mask[None] * displace / quad_dist[None]], axis=0
    ).astype(jnp.bfloat16)
    flat_smooth = smooth.reshape(1, -1)
    hidden_first = jnp.tanh(w_embed1[:, None] * flat_smooth + b_embed1[:, None])
    pre_second = (
        jnp.dot(w_embed2.T, hidden_first.astype(jnp.bfloat16), preferred_element_type=jnp.float32)
        + b_embed2[:, None]
    )
    tanh_second = jnp.tanh(pre_second)
    hidden_second = jnp.concatenate([hidden_first, hidden_first], axis=0) + tanh_second
    pre_third = (
        jnp.dot(w_embed3.T, hidden_second.astype(jnp.bfloat16), preferred_element_type=jnp.float32)
        + b_embed3[:, None]
    )
    tanh_third = jnp.tanh(pre_third)
    embedding = (jnp.concatenate([hidden_second, hidden_second], axis=0) + tanh_third).astype(
        jnp.bfloat16
    )
    embedding_width = embedding.shape[0]
    embedding_rows = embedding.reshape(embedding_width, blocks, slot_count)
    descriptor_tensor = (
        jnp.einsum(
            "srj,lrj->rsl", environment_matrix, embedding_rows, preferred_element_type=jnp.float32
        )
        / NEIGHBOUR_SLOTS
    )
    axis_part = descriptor_tensor[:, :, :M2]
    descriptor = jnp.einsum(
        "bce,bck->bek", descriptor_tensor, axis_part, precision=highest_precision
    )
    flat_descr = descriptor.reshape(blocks, -1).astype(jnp.bfloat16)
    fit_hidden = jnp.tanh(jnp.dot(flat_descr, w_fit1, preferred_element_type=jnp.float32) + b_fit1)
    pre_out = (
        jnp.dot(fit_hidden.astype(jnp.bfloat16), w_fit2, preferred_element_type=jnp.float32)
        + b_fit2
    )
    tanh_out = jnp.tanh(pre_out)
    energy = jnp.dot(fit_hidden + tanh_out, w_out, precision=highest_precision)
    grad_out = (w_out[None, :] * (1.0 - tanh_out * tanh_out)).astype(jnp.bfloat16)
    grad_fit = w_out[None, :] + jnp.dot(grad_out, w_fit2.T, preferred_element_type=jnp.float32)
    grad_act = (grad_fit * (1.0 - fit_hidden * fit_hidden)).astype(jnp.bfloat16)
    grad_descr = jnp.dot(grad_act, w_fit1.T, preferred_element_type=jnp.float32).reshape(
        blocks, embedding_width, -1
    )
    grad_tensor = jnp.einsum("bek,bck->bce", grad_descr, axis_part, precision=highest_precision)
    extra_grad = jnp.einsum(
        "bek,bce->bck", grad_descr, descriptor_tensor, precision=highest_precision
    )
    grad_tensor = grad_tensor + jnp.pad(
        extra_grad, ((0, 0), (0, 0), (0, embedding_width - extra_grad.shape[2]))
    )
    descriptor_product_gradient = grad_tensor.astype(jnp.bfloat16)
    environment_gradient = (
        jnp.einsum(
            "ohm,hdo->dhm",
            embedding_rows,
            descriptor_product_gradient,
            preferred_element_type=jnp.float32,
        )
        / NEIGHBOUR_SLOTS
    )
    embedding_gradient = (
        jnp.einsum(
            "zmj,mzr->rmj",
            environment_matrix,
            descriptor_product_gradient,
            preferred_element_type=jnp.float32,
        ).reshape(embedding_width, -1)
        / NEIGHBOUR_SLOTS
    )
    grad_third = (embedding_gradient * (1.0 - tanh_third * tanh_third)).astype(jnp.bfloat16)
    half_width = embedding_width // 2
    grad_hidden2 = (
        embedding_gradient[:half_width]
        + embedding_gradient[half_width:]
        + jnp.dot(w_embed3, grad_third, preferred_element_type=jnp.float32)
    )
    grad_second = (grad_hidden2 * (1.0 - tanh_second * tanh_second)).astype(jnp.bfloat16)
    quarter = half_width // 2
    grad_hidden1 = (
        grad_hidden2[:quarter]
        + grad_hidden2[quarter:]
        + jnp.dot(w_embed2, grad_second, preferred_element_type=jnp.float32)
    )
    grad_smooth = (
        jnp.dot(
            w_embed1,
            grad_hidden1 * (1.0 - hidden_first * hidden_first),
            precision=highest_precision,
        ).reshape(blocks, slot_count)
        + environment_gradient[0]
    )
    radial = jnp.sum(environment_gradient[1:] * displace, axis=0)
    factor = -grad_smooth / (radius * quad_dist) - 2.0 * radial / (quad_dist * quad_dist)
    pair_grad = live_mask[None] * (
        displace * factor[None] + environment_gradient[1:] / quad_dist[None]
    )
    return (energy, pair_grad)


def ghost_table(coords):
    stacked = coords[:, None, :]
    brick_pos = lax.all_gather(stacked, "help", axis=2, tiled=True)
    gathered = extended(brick_pos, (("brick", 1),), 1)
    return gathered.reshape(3, -1)


def return_forces(gathered):
    reduced = lax.psum_scatter(gathered, "help", scatter_dimension=2, tiled=True)
    padded = extended(reduced, (("brick", 1),), 1)
    returned = padded[:, 0] + padded[:, 2] + padded[:, 4]
    return returned


def evaluate(coords, neighbors, weights):
    ghost = ghost_table(coords)
    brick_len = ghost.shape[1] // 3
    atom_count = coords.shape[1]
    safe_index = jnp.maximum(neighbors, 0)
    live_mask = (neighbors >= 0).astype(jnp.float32)
    shift_x = (safe_index // brick_len - 1).astype(jnp.float32)
    block_size = 32
    block_count = atom_count // block_size

    def one_block(pieces):
        own_pos, table_index, offset, mask_rows = pieces
        neighbour_pos = jnp.take(ghost, table_index, axis=1)
        displace = neighbour_pos - own_pos[:, :, None]
        displace = (
            jnp.concatenate([displace[:1] + offset[None], displace[1:]], axis=0) * mask_rows[None]
        )
        return pair_terms(displace, mask_rows, weights)

    own_blocks = coords.reshape(3, block_count, block_size).transpose(1, 0, 2)
    energy, pair_grads = lax.map(
        one_block,
        (
            own_blocks,
            safe_index.reshape(block_count, block_size, -1),
            shift_x.reshape(block_count, block_size, -1),
            live_mask.reshape(block_count, block_size, -1),
        ),
    )
    pair_grads = pair_grads.transpose(1, 0, 2, 3).reshape(3, atom_count, -1)
    energy_rows = energy.reshape(-1)
    gathered = jnp.zeros((3, 3 * brick_len), jnp.float32).at[:, safe_index].add(pair_grads)
    returned = return_forces(gathered.reshape(3, 3, brick_len))
    return (energy_rows, jnp.sum(pair_grads, axis=2) - returned)


def local(
    positions,
    velocities,
    forces_in,
    neighbors,
    w_embed1,
    b_embed1,
    w_embed2,
    b_embed2,
    w_embed3,
    b_embed3,
    w_fit1,
    b_fit1,
    w_fit2,
    b_fit2,
    w_out,
):
    weights = (
        w_embed1,
        b_embed1,
        w_embed2,
        b_embed2,
        w_embed3,
        b_embed3,
        w_fit1,
        b_fit1,
        w_fit2,
        b_fit2,
        w_out,
    )
    coords = positions
    speed = velocities
    force_now = forces_in
    energy = jnp.zeros((positions.shape[1],), jnp.float32)
    for md_step in range(STEPS):
        speed = speed + kick_scale * force_now
        coords = coords + time_step * speed
        energy, force_now = evaluate(coords, neighbors, weights)
        speed = speed + kick_scale * force_now
    return (coords, speed, energy, force_now)


def solution(mesh):
    return jax.shard_map(
        local,
        mesh=mesh,
        in_specs=(
            P(None, ("brick", "help")),
            P(None, ("brick", "help")),
            P(None, ("brick", "help")),
            P(("brick", "help"), None),
            P(),
            P(),
            P(),
            P(),
            P(),
            P(),
            P(),
            P(),
            P(),
            P(),
            P(),
        ),
        out_specs=(
            P(None, ("brick", "help")),
            P(None, ("brick", "help")),
            P(("brick", "help")),
            P(None, ("brick", "help")),
        ),
        check_vma=False,
    )
```

profile of v0, /device:TPU:0, one launch (start us, length us, event | category | flops | bytes accessed | tf_op | source)
XLA Modules:
  0.0 359.1 jit_solution(11644134132301394717)
XLA Ops:
  7.9 13.6 %all-gather.2 = f32[4,64,3]{1,2,0:T(4,128)S(1)} all-gather(f32[1,64,3]{1,2,0:T(4,128)S(1)} %bitcast.479), channel_id=2, replica_groups=mesh['brick'=8,'help'=4] {'help'}, dimensions={0}, use_global_device_ids=true | all-gather | bytes 3840 | tf_op jit(solution)/shard_map/all_gather | solution.py:148
  22.9 1.4 fusion.116
  24.5 1.1 collective-permute-done
  26.5 71.5 %while.26 = (s32[]{:T(128)}, f32[2,3,32,128]{3,1,2,0:T(4,128)}, f32[2,32,128]{2,0,1:T(2,128)S(1)}, s32[2,32,128]{2,1,0:T(8,128)}, f32[3,768]{0,1:T(8,128)S(1)}, ...) while((s32[]{:T(128)}, f32[2,3,32,128]{3,1,2,0:T(4,128)}, ...), condition=%wide.region_3.5_spmd, body=%wide.region_0.4_spmd.sunk | while | flops 271267840 | bytes 53851500 | solution.py:180
  27.4 10.8 %gather_fusion = f32[4096,3]{1,0:T(8,128)S(1)} fusion(f32[3,768]{0,1:T(8,128)S(1)} %get-tuple-element.963, s32[4096]{0:T(1024)S(1)} %bitcast_clamp_fusion.4), kind=kCustom, calls=%fused_computation.clone.clone.1 | custom fusion | bytes 114688 | tf_op jit(solution)/shard_map/while/body/eval_jaxpr/jit(_take)/gather | solution.py:172
  40.7 2.1 maximum_add_fusion.6
  42.9 1.2 fusion.262
  47.2 1.2 copy.233
  48.5 1.4 fusion.265
  51.0 1.5 fusion.267
  52.5 1.8 copy.234
  54.3 1.4 fusion.268
  55.6 1.2 fusion.269
  57.8 1.4 fusion.271
  59.2 1.0 fusion.272
  60.4 1.1 fusion.273
  63.1 10.8 %gather_fusion = f32[4096,3]{1,0:T(8,128)S(1)} fusion(f32[3,768]{0,1:T(8,128)S(1)} %get-tuple-element.963, s32[4096]{0:T(1024)S(1)} %bitcast_clamp_fusion.4), kind=kCustom, calls=%fused_computation.clone.clone.1 | custom fusion | bytes 114688 | tf_op jit(solution)/shard_map/while/body/eval_jaxpr/jit(_take)/gather | solution.py:172
  76.5 2.1 maximum_add_fusion.6
  78.6 1.2 fusion.262
  83.0 1.2 copy.233
  84.2 1.4 fusion.265
  86.7 1.5 fusion.267
  88.3 1.8 copy.234
  90.0 1.4 fusion.268
  91.4 1.2 fusion.269
  93.5 1.4 fusion.271
  95.0 1.0 fusion.272
  96.1 1.1 fusion.273
  98.0 3.5 copy.144
  101.6 45.3 %scatter_custom_fusion = f32[3,768]{0,1:T(8,128)S(1)} fusion(s32[8192]{0:T(1024)} %get-tuple-element.670, f32[8192,3]{1,0:T(8,128)} %bitcast.458, f32[]{:T(128)} %constant.160.clone.1), kind=kCustom, calls=%fused_computation.189 | custom fusion | flops 24576 | bytes 9728 | tf_op jit(solution)/shard_map/scatter-add | solution.py:191
  148.1 24.3 %reduce-scatter.7.cloned.1.call-done = f32[64,9]{1,0:T(8,128)} async-done(((f32[256,9]{1,0:T(8,128)}), f32[64,9]{1,0:T(8,128)}) %reduce-scatter.7.cloned.1.call-update) | async-done | bytes 2320
  174.7 2.7 collective-permute-done.2
  178.0 11.9 %all-gather.3 = f32[4,64,3]{1,2,0:T(4,128)S(1)} all-gather(f32[1,64,3]{1,2,0:T(4,128)S(1)} %bitcast.480), channel_id=3, replica_groups=mesh['brick'=8,'help'=4] {'help'}, dimensions={0}, use_global_device_ids=true | all-gather | bytes 3840 | tf_op jit(solution)/shard_map/all_gather | solution.py:148
  191.4 2.8 collective-permute-done.4
  195.8 77.6 %while.27 = (s32[]{:T(128)}, f32[2,32]{1,0:T(2,128)}, f32[2,3,32,128]{3,1,2,0:T(4,128)}, f32[2,32,128]{2,0,1:T(2,128)S(1)}, s32[2,32,128]{2,1,0:T(8,128)}, /*ind...) while((s32[]{:T(128)}, f32[2,32]{1,0:T(2,128)}, ...), condition=%wide.region_10.12_spmd, body=%wide.region_7.11_spmd.sunk | while | flops 271367680 | bytes 45020100 | solution.py:180
  196.6 11.8 %gather_fusion.1 = f32[4096,3]{1,0:T(8,128)S(1)} fusion(f32[3,768]{0,1:T(8,128)} %get-tuple-element.1025, s32[4096]{0:T(1024)S(1)} %bitcast_clamp_fusion.5), kind=kCustom, calls=%fused_computation.1.clone.clone.1 | custom fusion | bytes 114688 | tf_op jit(solution)/shard_map/while/body/eval_jaxpr/jit(_take)/gather | solution.py:172
  211.0 2.1 maximum_add_fusion.7
  213.1 1.2 fusion.301
  217.4 1.2 copy.241
  218.7 1.4 fusion.304
  221.1 1.3 dynamic_update_slice.27
  222.4 2.4 fusion.307
  224.7 1.7 copy.242
  227.3 1.6 fusion.310
  228.9 1.3 multiply_bitcast_fusion.7
  230.2 1.4 fusion.311
  232.8 1.1 fusion.313
  235.4 11.8 %gather_fusion.1 = f32[4096,3]{1,0:T(8,128)S(1)} fusion(f32[3,768]{0,1:T(8,128)} %get-tuple-element.1025, s32[4096]{0:T(1024)S(1)} %bitcast_clamp_fusion.5), kind=kCustom, calls=%fused_computation.1.clone.clone.1 | custom fusion | bytes 114688 | tf_op jit(solution)/shard_map/while/body/eval_jaxpr/jit(_take)/gather | solution.py:172
  249.7 2.1 maximum_add_fusion.7
  251.8 1.2 fusion.301
  256.2 1.2 copy.241
  257.4 1.4 fusion.304
  259.9 1.3 dynamic_update_slice.27
  261.1 2.4 fusion.307
  263.5 1.7 copy.242
  266.1 1.6 fusion.310
  267.7 1.3 multiply_bitcast_fusion.7
  269.0 1.4 fusion.311
  271.6 1.1 fusion.313
  273.4 3.5 copy.152
  276.9 45.2 %scatter_custom_fusion.1 = f32[3,768]{0,1:T(8,128)S(1)} fusion(s32[8192]{0:T(1024)} %get-tuple-element.670, f32[8192,3]{1,0:T(8,128)} %bitcast.457, f32[]{:T(128)} %constant.160.clone.1), kind=kCustom, calls=%fused_computation.187 | custom fusion | flops 24576 | bytes 9728 | tf_op jit(solution)/shard_map/scatter-add | solution.py:191
  323.3 23.3 %reduce-scatter.9.cloned.1.call-done = f32[64,9]{1,0:T(8,128)} async-done(((f32[256,9]{1,0:T(8,128)}), f32[64,9]{1,0:T(8,128)}) %reduce-scatter.9.cloned.1.call-update) | async-done | bytes 2320
  348.5 1.3 reshape.307
  349.8 1.8 collective-permute-done.6
  (385 shorter events, 52.5 us)
Async XLA Ops:
  7.2 165.2 %reduce-scatter.7.cloned.1.call-start = ((), (), s32[]{:S(2)}) async-start(), calls=%async_computation.2 | async-start | bytes 163840
  7.9 18.6 %copy-start.58 = (f32[3,64]{1,0:T(4,128)}, f32[3,64]{1,0:T(4,128)S(1)}, u32[]{:S(2)}) copy-start(f32[3,64]{1,0:T(4,128)S(1)} %multiply_add_fusion.2) | copy-start | bytes 2308
  21.6 2.8 collective-permute-start.1
  21.7 4.0 %collective-permute-start = (f32[3,1,256]{2,0,1:T(4,128)S(1)}, f32[3,1,256]{2,0,1:T(4,128)S(1)}, u32[]{:S(2)}, u32[]{:S(2)}) collective-permute-start(f32[3,1,256]{2,0,1:T(4,128)S(1)} %bitcast.482), channel_id=1, source_target_pairs={{0,4},{4,8},{8,12},{12,16},{16,20},{20,24},{24,28},{28,0},{1,5},{5... | collective-permute-start | bytes 9224 | tf_op jit(solution)/shard_map/ppermute | solution.py:21
  26.5 16.3 %copy-start.14 = (f32[3,768]{0,1:T(8,128)}, f32[3,768]{0,1:T(8,128)S(1)}, u32[]{:S(2)}) copy-start(f32[3,768]{0,1:T(8,128)S(1)} %get-tuple-element.963) | copy-start | bytes 27652 | tf_op jit(solution)/shard_map/while
  26.5 16.3 %copy-start.36 = (f32[2,32,128]{2,0,1:T(2,128)}, f32[2,32,128]{2,0,1:T(2,128)S(1)}, u32[]{:S(2)}) copy-start(f32[2,32,128]{2,0,1:T(2,128)S(1)} %get-tuple-element.961) | copy-start | bytes 98308 | tf_op jit(solution)/shard_map/while
  26.5 16.3 %copy-start.40 = (f32[2,32,128]{2,0,1:T(2,128)}, f32[2,32,128]{2,0,1:T(2,128)S(1)}, u32[]{:S(2)}) copy-start(f32[2,32,128]{2,0,1:T(2,128)S(1)} %get-tuple-element.965) | copy-start | bytes 98308 | tf_op jit(solution)/shard_map/while
  26.5 16.3 %copy-start.56 = (f32[2,3,32]{2,1,0:T(4,128)}, f32[2,3,32]{2,1,0:T(4,128)S(1)}, u32[]{:S(2)}) copy-start(f32[2,3,32]{2,1,0:T(4,128)S(1)} %get-tuple-element.964) | copy-start | bytes 2308 | tf_op jit(solution)/shard_map/while
  26.5 14.2 %copy-start.34 = (bf16[32,64]{1,0:T(8,128)(2,1)S(1)}, bf16[32,64]{1,0:T(8,128)(2,1)}, u32[]{:S(2)}) copy-start(bf16[32,64]{1,0:T(8,128)(2,1)} %get-tuple-element.968) | copy-start | bytes 12292 | tf_op jit(solution)/shard_map/while
  39.7 4.6 %copy-start.18 = (f32[1,32,128]{2,0,1:T(1,128)}, f32[1,32,128]{2,0,1:T(1,128)S(1)}, u32[]{:S(2)}) copy-start(f32[1,32,128]{2,0,1:T(1,128)S(1)} %get-tuple-element.891) | copy-start | bytes 49156 | tf_op jit(solution)/shard_map/while
  39.8 4.6 %copy-start.12 = (f32[2,32,128]{2,0,1:T(2,128)}, f32[2,32,128]{2,0,1:T(2,128)S(1)}, u32[]{:S(2)}) copy-start(f32[2,32,128]{2,0,1:T(2,128)S(1)} %slice.243) | copy-start | bytes 98308 | tf_op jit(solution)/shard_map/while
  39.9 4.2 %copy-start.25 = (f32[4096]{0:T(1024)}, f32[4096]{0:T(1024)S(1)}, u32[]{:S(2)}) copy-start(f32[4096]{0:T(1024)S(1)} %bitcast_multiply_fusion.6) | copy-start | bytes 49156 | tf_op jit(solution)/shard_map/while
  44.3 4.1 %copy-start = (bf16[2048,240]{0,1:T(8,128)(2,1)S(1)}, bf16[2048,240]{0,1:T(8,128)(2,1)}, u32[]{:S(2)}) copy-start(bf16[2048,240]{0,1:T(8,128)(2,1)} %get-tuple-element.973) | copy-start | bytes 2949124 | tf_op jit(solution)/shard_map/while
  44.3 5.6 %copy-start.7 = (bf16[240,240]{1,0:T(8,128)(2,1)S(1)}, bf16[240,240]{1,0:T(8,128)(2,1)}, u32[]{:S(2)}) copy-start(bf16[240,240]{1,0:T(8,128)(2,1)} %get-tuple-element.975) | copy-start | bytes 345604 | tf_op jit(solution)/shard_map/while
  44.3 5.6 %copy-start.50 = (f32[240]{0:T(256)S(1)}, f32[240]{0:T(256)}, u32[]{:S(2)}) copy-start(f32[240]{0:T(256)} %get-tuple-element.976) | copy-start | bytes 2884 | tf_op jit(solution)/shard_map/while
  46.5 4.4 %copy-start.9 = (f32[32,4,128]{2,1,0:T(4,128)}, f32[32,4,128]{2,1,0:T(4,128)S(1)}, u32[]{:S(2)}) copy-start(f32[32,4,128]{2,1,0:T(4,128)S(1)} %convolution_multiply_fusion.6) | copy-start | bytes 196612 | tf_op jit(solution)/shard_map/while
  52.5 4.3 %copy-start.4 = (bf16[16,32,8,128]{3,2,1,0:T(8,128)(2,1)S(1)}, bf16[16,32,8,128]{3,2,1,0:T(8,128)(2,1)}, u32[]{:S(2)}) copy-start(bf16[16,32,8,128]{3,2,1,0:T(8,128)(2,1)} %copy-done.3) | copy-start | bytes 3145732 | tf_op jit(solution)/shard_map/while
  52.5 4.7 %copy-start.22 = (bf16[3,32,128]{2,0,1:T(4,128)(2,1)S(1)}, bf16[3,32,128]{2,0,1:T(4,128)(2,1)}, u32[]{:S(2)}) copy-start(bf16[3,32,128]{2,0,1:T(4,128)(2,1)} %copy-done.21) | copy-start | bytes 73732 | tf_op jit(solution)/shard_map/while
  52.5 4.7 %copy-start.33 = (bf16[1,32,128]{2,0,1:T(2,128)(2,1)S(1)}, bf16[1,32,128]{2,0,1:T(2,128)(2,1)}, u32[]{:S(2)}) copy-start(bf16[1,32,128]{2,0,1:T(2,128)(2,1)} %copy-done.32) | copy-start | bytes 24580 | tf_op jit(solution)/shard_map/while
  62.3 16.3 %copy-start.14 = (f32[3,768]{0,1:T(8,128)}, f32[3,768]{0,1:T(8,128)S(1)}, u32[]{:S(2)}) copy-start(f32[3,768]{0,1:T(8,128)S(1)} %get-tuple-element.963) | copy-start | bytes 27652 | tf_op jit(solution)/shard_map/while
  62.3 16.3 %copy-start.36 = (f32[2,32,128]{2,0,1:T(2,128)}, f32[2,32,128]{2,0,1:T(2,128)S(1)}, u32[]{:S(2)}) copy-start(f32[2,32,128]{2,0,1:T(2,128)S(1)} %get-tuple-element.961) | copy-start | bytes 98308 | tf_op jit(solution)/shard_map/while
  62.3 16.3 %copy-start.40 = (f32[2,32,128]{2,0,1:T(2,128)}, f32[2,32,128]{2,0,1:T(2,128)S(1)}, u32[]{:S(2)}) copy-start(f32[2,32,128]{2,0,1:T(2,128)S(1)} %get-tuple-element.965) | copy-start | bytes 98308 | tf_op jit(solution)/shard_map/while
  62.3 16.3 %copy-start.56 = (f32[2,3,32]{2,1,0:T(4,128)}, f32[2,3,32]{2,1,0:T(4,128)S(1)}, u32[]{:S(2)}) copy-start(f32[2,3,32]{2,1,0:T(4,128)S(1)} %get-tuple-element.964) | copy-start | bytes 2308 | tf_op jit(solution)/shard_map/while
  62.3 14.2 %copy-start.34 = (bf16[32,64]{1,0:T(8,128)(2,1)S(1)}, bf16[32,64]{1,0:T(8,128)(2,1)}, u32[]{:S(2)}) copy-start(bf16[32,64]{1,0:T(8,128)(2,1)} %get-tuple-element.968) | copy-start | bytes 12292 | tf_op jit(solution)/shard_map/while
  75.5 4.6 %copy-start.18 = (f32[1,32,128]{2,0,1:T(1,128)}, f32[1,32,128]{2,0,1:T(1,128)S(1)}, u32[]{:S(2)}) copy-start(f32[1,32,128]{2,0,1:T(1,128)S(1)} %get-tuple-element.891) | copy-start | bytes 49156 | tf_op jit(solution)/shard_map/while
  75.5 4.6 %copy-start.12 = (f32[2,32,128]{2,0,1:T(2,128)}, f32[2,32,128]{2,0,1:T(2,128)S(1)}, u32[]{:S(2)}) copy-start(f32[2,32,128]{2,0,1:T(2,128)S(1)} %slice.243) | copy-start | bytes 98308 | tf_op jit(solution)/shard_map/while
  75.6 4.2 %copy-start.25 = (f32[4096]{0:T(1024)}, f32[4096]{0:T(1024)S(1)}, u32[]{:S(2)}) copy-start(f32[4096]{0:T(1024)S(1)} %bitcast_multiply_fusion.6) | copy-start | bytes 49156 | tf_op jit(solution)/shard_map/while
  80.1 5.6 %copy-start.7 = (bf16[240,240]{1,0:T(8,128)(2,1)S(1)}, bf16[240,240]{1,0:T(8,128)(2,1)}, u32[]{:S(2)}) copy-start(bf16[240,240]{1,0:T(8,128)(2,1)} %get-tuple-element.975) | copy-start | bytes 345604 | tf_op jit(solution)/shard_map/while
  80.1 5.6 %copy-start.50 = (f32[240]{0:T(256)S(1)}, f32[240]{0:T(256)}, u32[]{:S(2)}) copy-start(f32[240]{0:T(256)} %get-tuple-element.976) | copy-start | bytes 2884 | tf_op jit(solution)/shard_map/while
  82.3 4.4 %copy-start.9 = (f32[32,4,128]{2,1,0:T(4,128)}, f32[32,4,128]{2,1,0:T(4,128)S(1)}, u32[]{:S(2)}) copy-start(f32[32,4,128]{2,1,0:T(4,128)S(1)} %convolution_multiply_fusion.6) | copy-start | bytes 196612 | tf_op jit(solution)/shard_map/while
  88.2 4.3 %copy-start.4 = (bf16[16,32,8,128]{3,2,1,0:T(8,128)(2,1)S(1)}, bf16[16,32,8,128]{3,2,1,0:T(8,128)(2,1)}, u32[]{:S(2)}) copy-start(bf16[16,32,8,128]{3,2,1,0:T(8,128)(2,1)} %copy-done.3) | copy-start | bytes 3145732 | tf_op jit(solution)/shard_map/while
  88.3 4.7 %copy-start.22 = (bf16[3,32,128]{2,0,1:T(4,128)(2,1)S(1)}, bf16[3,32,128]{2,0,1:T(4,128)(2,1)}, u32[]{:S(2)}) copy-start(bf16[3,32,128]{2,0,1:T(4,128)(2,1)} %copy-done.21) | copy-start | bytes 73732 | tf_op jit(solution)/shard_map/while
  88.3 4.7 %copy-start.33 = (bf16[1,32,128]{2,0,1:T(2,128)(2,1)S(1)}, bf16[1,32,128]{2,0,1:T(2,128)(2,1)}, u32[]{:S(2)}) copy-start(bf16[1,32,128]{2,0,1:T(2,128)(2,1)} %copy-done.32) | copy-start | bytes 24580 | tf_op jit(solution)/shard_map/while
  101.5 72.5 %copy-start.49 = (f32[2,3,32,128]{3,1,2,0:T(4,128)S(1)}, f32[2,3,32,128]{3,1,2,0:T(4,128)}, u32[]{:S(2)}) copy-start(f32[2,3,32,128]{3,1,2,0:T(4,128)} %get-tuple-element.460) | copy-start | bytes 294916
  101.5 75.9 %copy-start.59 = (f32[3,64]{1,0:T(4,128)S(1)}, f32[3,64]{1,0:T(4,128)}, u32[]{:S(2)}) copy-start(f32[3,64]{1,0:T(4,128)} %copy-done.58) | copy-start | bytes 2308
  101.5 75.9 %copy-start.62 = (f32[3,64]{1,0:T(4,128)S(1)}, f32[3,64]{1,0:T(4,128)}, u32[]{:S(2)}) copy-start(f32[3,64]{1,0:T(4,128)} %param.22) | copy-start | bytes 2308
  101.5 75.9 %copy-start.63 = (f32[3,64]{1,0:T(4,128)S(1)}, f32[3,64]{1,0:T(4,128)}, u32[]{:S(2)}) copy-start(f32[3,64]{1,0:T(4,128)} %param.23) | copy-start | bytes 2308
  101.5 94.3 %copy-start.1 = (bf16[2048,240]{0,1:T(8,128)(2,1)S(1)}, bf16[2048,240]{0,1:T(8,128)(2,1)}, u32[]{:S(2)}) copy-start(bf16[2048,240]{0,1:T(8,128)(2,1)} %get-tuple-element.1043) | copy-start | bytes 2949124
  101.5 94.3 %copy-start.8 = (bf16[240,240]{1,0:T(8,128)(2,1)S(1)}, bf16[240,240]{1,0:T(8,128)(2,1)}, u32[]{:S(2)}) copy-start(bf16[240,240]{1,0:T(8,128)(2,1)} %get-tuple-element.1044) | copy-start | bytes 345604
  101.5 94.3 %copy-start.35 = (bf16[32,64]{1,0:T(8,128)(2,1)S(1)}, bf16[32,64]{1,0:T(8,128)(2,1)}, u32[]{:S(2)}) copy-start(bf16[32,64]{1,0:T(8,128)(2,1)} %get-tuple-element.1045) | copy-start | bytes 12292
  148.0 198.6 %reduce-scatter.9.cloned.1.call-start = ((), (), s32[]{:S(2)}) async-start(), calls=%async_computation.3 | async-start | bytes 163840
  173.4 1.3 collective-permute-start.3
  173.5 3.9 %collective-permute-start.2 = (f32[3,1,64]{2,0,1:T(4,128)S(1)}, f32[3,1,64]{2,0,1:T(4,128)S(1)}, u32[]{:S(2)}, u32[]{:S(2)}) collective-permute-start(f32[3,1,64]{2,0,1:T(4,128)S(1)} %copy.169), channel_id=1, source_target_pairs={{0,4},{4,8},{8,12},{12,16},{16,20},{20,24},{24,28},{28,0},{1,5},{5... | collective-permute-start | bytes 2312 | tf_op jit(solution)/shard_map/ppermute | solution.py:21
  178.0 17.8 %copy-start.60 = (f32[3,64]{1,0:T(4,128)}, f32[3,64]{1,0:T(4,128)S(1)}, u32[]{:S(2)}) copy-start(f32[3,64]{1,0:T(4,128)S(1)} %get-tuple-element.650) | copy-start | bytes 2308
  190.0 1.3 collective-permute-start.5
  190.0 4.2 %collective-permute-start.4 = (f32[3,1,256]{2,0,1:T(4,128)S(1)}, f32[3,1,256]{2,0,1:T(4,128)S(1)}, u32[]{:S(2)}, u32[]{:S(2)}) collective-permute-start(f32[3,1,256]{2,0,1:T(4,128)S(1)} %bitcast.485), channel_id=1, source_target_pairs={{0,4},{4,8},{8,12},{12,16},{16,20},{20,24},{24,28},{28,0},{1,5},{5... | collective-permute-start | bytes 9224 | tf_op jit(solution)/shard_map/ppermute | solution.py:21
  195.8 13.3 %copy-start.54 = (f32[2,3,32]{2,1,0:T(4,128)}, f32[2,3,32]{2,1,0:T(4,128)S(1)}, u32[]{:S(2)}) copy-start(f32[2,3,32]{2,1,0:T(4,128)S(1)} %get-tuple-element.1026) | copy-start | bytes 2308 | tf_op jit(solution)/shard_map/while
  195.8 17.2 %copy-start.38 = (f32[2,32,128]{2,0,1:T(2,128)}, f32[2,32,128]{2,0,1:T(2,128)S(1)}, u32[]{:S(2)}) copy-start(f32[2,32,128]{2,0,1:T(2,128)S(1)} %get-tuple-element.1023) | copy-start | bytes 98308 | tf_op jit(solution)/shard_map/while
  195.9 17.2 %copy-start.42 = (f32[2,32,128]{2,0,1:T(2,128)}, f32[2,32,128]{2,0,1:T(2,128)S(1)}, u32[]{:S(2)}) copy-start(f32[2,32,128]{2,0,1:T(2,128)S(1)} %get-tuple-element.1027) | copy-start | bytes 98308 | tf_op jit(solution)/shard_map/while
  210.0 4.6 %copy-start.16 = (f32[1,32,128]{2,0,1:T(1,128)}, f32[1,32,128]{2,0,1:T(1,128)S(1)}, u32[]{:S(2)}) copy-start(f32[1,32,128]{2,0,1:T(1,128)S(1)} %get-tuple-element.916) | copy-start | bytes 49156 | tf_op jit(solution)/shard_map/while
  210.0 4.5 %copy-start.10 = (f32[2,32,128]{2,0,1:T(2,128)}, f32[2,32,128]{2,0,1:T(2,128)S(1)}, u32[]{:S(2)}) copy-start(f32[2,32,128]{2,0,1:T(2,128)S(1)} %slice.255) | copy-start | bytes 98308 | tf_op jit(solution)/shard_map/while
  210.1 4.2 %copy-start.23 = (f32[4096]{0:T(1024)}, f32[4096]{0:T(1024)S(1)}, u32[]{:S(2)}) copy-start(f32[4096]{0:T(1024)S(1)} %bitcast_multiply_fusion.7) | copy-start | bytes 49156 | tf_op jit(solution)/shard_map/while
  214.5 5.6 %copy-start.51 = (f32[240]{0:T(256)S(1)}, f32[240]{0:T(256)}, u32[]{:S(2)}) copy-start(f32[240]{0:T(256)} %get-tuple-element.1037) | copy-start | bytes 2884 | tf_op jit(solution)/shard_map/while
  234.6 13.2 %copy-start.54 = (f32[2,3,32]{2,1,0:T(4,128)}, f32[2,3,32]{2,1,0:T(4,128)S(1)}, u32[]{:S(2)}) copy-start(f32[2,3,32]{2,1,0:T(4,128)S(1)} %get-tuple-element.1026) | copy-start | bytes 2308 | tf_op jit(solution)/shard_map/while
  234.6 17.2 %copy-start.38 = (f32[2,32,128]{2,0,1:T(2,128)}, f32[2,32,128]{2,0,1:T(2,128)S(1)}, u32[]{:S(2)}) copy-start(f32[2,32,128]{2,0,1:T(2,128)S(1)} %get-tuple-element.1023) | copy-start | bytes 98308 | tf_op jit(solution)/shard_map/while
  234.7 17.2 %copy-start.42 = (f32[2,32,128]{2,0,1:T(2,128)}, f32[2,32,128]{2,0,1:T(2,128)S(1)}, u32[]{:S(2)}) copy-start(f32[2,32,128]{2,0,1:T(2,128)S(1)} %get-tuple-element.1027) | copy-start | bytes 98308 | tf_op jit(solution)/shard_map/while
  248.8 4.6 %copy-start.16 = (f32[1,32,128]{2,0,1:T(1,128)}, f32[1,32,128]{2,0,1:T(1,128)S(1)}, u32[]{:S(2)}) copy-start(f32[1,32,128]{2,0,1:T(1,128)S(1)} %get-tuple-element.916) | copy-start | bytes 49156 | tf_op jit(solution)/shard_map/while
  248.8 4.5 %copy-start.10 = (f32[2,32,128]{2,0,1:T(2,128)}, f32[2,32,128]{2,0,1:T(2,128)S(1)}, u32[]{:S(2)}) copy-start(f32[2,32,128]{2,0,1:T(2,128)S(1)} %slice.255) | copy-start | bytes 98308 | tf_op jit(solution)/shard_map/while
  248.9 4.2 %copy-start.23 = (f32[4096]{0:T(1024)}, f32[4096]{0:T(1024)S(1)}, u32[]{:S(2)}) copy-start(f32[4096]{0:T(1024)S(1)} %bitcast_multiply_fusion.7) | copy-start | bytes 49156 | tf_op jit(solution)/shard_map/while
  253.3 5.6 %copy-start.51 = (f32[240]{0:T(256)S(1)}, f32[240]{0:T(256)}, u32[]{:S(2)}) copy-start(f32[240]{0:T(256)} %get-tuple-element.1037) | copy-start | bytes 2884 | tf_op jit(solution)/shard_map/while
  276.9 71.3 %copy-start.46 = (f32[2,3,32,128]{3,1,2,0:T(4,128)S(1)}, f32[2,3,32,128]{3,1,2,0:T(4,128)}, u32[]{:S(2)}) copy-start(f32[2,3,32,128]{3,1,2,0:T(4,128)} %get-tuple-element.461) | copy-start | bytes 294916
  276.9 74.7 %copy-start.61 = (f32[3,64]{1,0:T(4,128)S(1)}, f32[3,64]{1,0:T(4,128)}, u32[]{:S(2)}) copy-start(f32[3,64]{1,0:T(4,128)} %get-tuple-element.651) | copy-start | bytes 2308
  347.7 2.2 collective-permute-start.7
  347.7 3.9 %collective-permute-start.6 = (f32[3,1,64]{2,0,1:T(4,128)S(1)}, f32[3,1,64]{2,0,1:T(4,128)S(1)}, u32[]{:S(2)}, u32[]{:S(2)}) collective-permute-start(f32[3,1,64]{2,0,1:T(4,128)S(1)} %copy.172), channel_id=1, source_target_pairs={{0,4},{4,8},{8,12},{12,16},{16,20},{20,24},{24,28},{28,0},{1,5},{5... | collective-permute-start | bytes 2312 | tf_op jit(solution)/shard_map/ppermute | solution.py:21
  (63 other events, 113.3 us)
Sparse Core Ops, SparseCore 0:
  148.2 24.1 reduce-scatter.6
  323.5 23.1 reduce-scatter.8
where the time goes:
time: 362 us; the launch traced here: 359 us
  other arithmetic  107 us (30%)
  local copies, waits for them, and re-layouts  87 us (24%)
  matrix products  64.1 us (18%)
  waiting for transfers between devices  57.3 us (16%)
  blocking collectives  25.5 us (7%)
  between operations  14.2 us (4%)
    scatter-add x2, other arithmetic, evaluate(): jnp.zeros((3, 3 * brick_len), jnp.float32).at[:, safe_index].add(pair_grads)  90.5 us
    unnamed x4, waiting for transfers between devices  47.6 us
    gather x8, local copies, waits for them, and re-layouts, one_block(): neighbour_pos = jnp.take(ghost, table_index, axis=1)  47.5 us
    all_gather x2, blocking collectives, ghost_table(): brick_pos = lax.all_gather(stacked, 'help', axis=2, tiled=True)  25.5 us
    while x212, local copies, waits for them, and re-layouts  8.73 us
    ppermute x4, waiting for transfers between devices, extended(): before = lax.ppermute(last, axis, up)  8.48 us
    dot_general x4, matrix products, pair_terms(): jnp.dot(w_embed2.T, hidden_first.astype(jnp.bfloat16), preferred_element_...  8.38 us
    dot_general x4, matrix products, pair_terms(): jnp.dot(grad_act, w_fit1.T, preferred_element_type=jnp.float32)  7.82 us
  transfers between devices with their start and end apart: 10, of which 8 were waited for; matrix products, arithmetic and copies ran while one was open for 1% of the time, Pallas kernels for 0%

commit v1 on v0

--- a/solution.py
+++ b/solution.py
@@ -9,6 +9,12 @@
 kick_scale = 0.25
 time_step = 0.05
 highest_precision = lax.Precision.HIGHEST
+
+
+def laid_out(parts, dim):
+    shape = list(parts.shape[1:])
+    shape[dim] *= parts.shape[0]
+    return jnp.moveaxis(parts, 0, dim).reshape(shape)
 
 
 def extended(value, sides, width):
@@ -145,7 +151,19 @@
 
 def ghost_table(coords):
     stacked = coords[:, None, :]
-    brick_pos = lax.all_gather(stacked, "help", axis=2, tiled=True)
+    length_2 = lax.axis_size("help")
+    pairs = [(i_2, (i_2 + 1) % length_2) for i_2 in range(length_2)]
+    back = [(b, a) for a, b in pairs]
+    lower, upper = ([], [])
+    for step in range(length_2 - 1):
+        if step % 2 == 0:
+            lower.append(lax.ppermute(lower[-1] if lower else stacked, "help", pairs))
+        else:
+            upper.append(lax.ppermute(upper[-1] if upper else stacked, "help", back))
+    blocks_2 = jnp.stack([*lower[::-1], stacked, *upper])
+    shift = lax.axis_index("help") - len(lower)
+    blocks_2 = blocks_2[(jnp.arange(length_2) - shift) % length_2]
+    brick_pos = laid_out(blocks_2, 2)
     gathered = extended(brick_pos, (("brick", 1),), 1)
     return gathered.reshape(3, -1)
 

time: 362 us -> 362 us (level)
  blocking collectives: 25.5 us -> 0 us
  waiting for transfers between devices: 57.3 us -> 72.9 us
  starting transfers between devices: 2.13 us -> 11 us
    all_gather x2 -> x0, blocking collectives: 25.5 us -> none  [ghost_table(): brick_pos = lax.all_gather(stacked, 'help', axis=2, tiled=True)]
    ppermute x0 -> x6, waiting for transfers between devices: none -> 16.9 us  [the longest x4 16.9 us: ghost_table(): lower.append(lax.ppermute(lower[-1] if lower else stacked, 'help', pairs))]
    ppermute x0 -> x6, starting transfers between devices: none -> 8.91 us  [the longest x2 8.9 us: ghost_table(): upper.append(lax.ppermute(upper[-1] if upper else stacked, 'help', back))]
  transfers between devices with their start and end apart: 10 -> 16, of which waited for: 8 -> 12; matrix products, arithmetic and copies ran while one was open for 1% -> 1% of each run, Pallas kernels for 0% -> 0%
where the time goes in v1:
time: 362 us; the launch traced here: 359 us
  other arithmetic  107 us (30%)
  local copies, waits for them, and re-layouts  88.1 us (24%)
  waiting for transfers between devices  72.9 us (20%)
  matrix products  64 us (18%)
  between operations  14.3 us (4%)
  starting transfers between devices  11 us (3%)
    scatter-add x2, other arithmetic, evaluate(): jnp.zeros((3, 3 * brick_len), jnp.float32).at[:, safe_index].add(pair_grads)  90.5 us
    gather x8, local copies, waits for them, and re-layouts, one_block(): neighbour_pos = jnp.take(ghost, table_index, axis=1)  47.5 us
    unnamed x4, waiting for transfers between devices  45.8 us
    ppermute x4, waiting for transfers between devices, ghost_table(): lower.append(lax.ppermute(lower[-1] if lower else stacked, 'help', pairs))  16.9 us
    ppermute x4, waiting for transfers between devices, extended(): before = lax.ppermute(last, axis, up)  9.05 us
    ppermute x2, starting transfers between devices, ghost_table(): upper.append(lax.ppermute(upper[-1] if upper else stacked, 'help', back))  8.9 us
    while x212, local copies, waits for them, and re-layouts  8.66 us
    dot_general x4, matrix products, pair_terms(): jnp.dot(w_embed2.T, hidden_first.astype(jnp.bfloat16), preferred_element_...  8.31 us
  transfers between devices with their start and end apart: 16, of which 12 were waited for; matrix products, arithmetic and copies ran while one was open for 1% of the time, Pallas kernels for 0%

profile of v1, /device:TPU:0, one launch (start us, length us, event | category | flops | bytes accessed | tf_op | source)
XLA Modules:
  0.0 359.2 jit_solution(9308263108978907586)
XLA Ops:
  7.9 5.1 %collective-permute-start.2 = (f32[3,1,64]{2,0,1:T(4,128)S(1)}, f32[3,1,64]{2,0,1:T(4,128)S(1)}, u32[]{:S(2)}, u32[]{:S(2)}) collective-permute-start(f32[3,1,64]{2,0,1:T(4,128)S(1)} %bitcast.487), channel_id=1, source_target_pairs={{1,0},{2,1},{3,2},{0,3},{5,4},{6,5},{7,6},{4,7},{9,8},{10,9},{11,1... | collective-permute-start | bytes 2312 | tf_op jit(solution)/shard_map/ppermute | solution.py:162
  13.8 4.6 %collective-permute-done = f32[3,1,64]{2,0,1:T(4,128)S(1)} collective-permute-done((f32[3,1,64]{2,0,1:T(4,128)S(1)}, f32[3,1,64]{2,0,1:T(4,128)S(1)}, u32[]{:S(2)}, u32[]{:S(2)}) %collective-permute-start) | collective-permute-done | bytes 800 | tf_op jit(solution)/shard_map/ppermute | solution.py:160
  18.4 5.4 %collective-permute-done.1 = f32[3,1,64]{2,0,1:T(4,128)S(1)} collective-permute-done((f32[3,1,64]{2,0,1:T(4,128)S(1)}, f32[3,1,64]{2,0,1:T(4,128)S(1)}, u32[]{:S(2)}, u32[]{:S(2)}) %collective-permute-start.1) | collective-permute-done | bytes 800 | tf_op jit(solution)/shard_map/ppermute | solution.py:160
  25.0 1.4 fusion.118
  26.5 1.9 collective-permute-done.3
  29.3 71.4 %while.26 = (s32[]{:T(128)}, f32[2,3,32,128]{3,1,2,0:T(4,128)}, f32[2,32,128]{2,0,1:T(2,128)S(1)}, s32[2,32,128]{2,1,0:T(8,128)}, f32[3,768]{0,1:T(8,128)S(1)}, ...) while((s32[]{:T(128)}, f32[2,3,32,128]{3,1,2,0:T(4,128)}, ...), condition=%wide.region_3.5_spmd, body=%wide.region_0.4_spmd.sunk | while | flops 271267840 | bytes 53851500 | solution.py:198
  30.2 10.8 %gather_fusion = f32[4096,3]{1,0:T(8,128)S(1)} fusion(f32[3,768]{0,1:T(8,128)S(1)} %get-tuple-element.926, s32[4096]{0:T(1024)S(1)} %bitcast_clamp_fusion.4), kind=kCustom, calls=%fused_computation.clone.clone.1 | custom fusion | bytes 114688 | tf_op jit(solution)/shard_map/while/body/eval_jaxpr/jit(_take)/gather | solution.py:190
  43.5 2.1 maximum_add_fusion.6
  45.6 1.2 fusion.264
  50.0 1.2 copy.199
  51.2 1.4 fusion.267
  53.7 1.5 fusion.269
  55.3 1.8 copy.200
  57.0 1.4 fusion.270
  58.4 1.2 fusion.271
  60.5 1.4 fusion.273
  65.9 10.8 %gather_fusion = f32[4096,3]{1,0:T(8,128)S(1)} fusion(f32[3,768]{0,1:T(8,128)S(1)} %get-tuple-element.926, s32[4096]{0:T(1024)S(1)} %bitcast_clamp_fusion.4), kind=kCustom, calls=%fused_computation.clone.clone.1 | custom fusion | bytes 114688 | tf_op jit(solution)/shard_map/while/body/eval_jaxpr/jit(_take)/gather | solution.py:190
  79.2 2.1 maximum_add_fusion.6
  81.3 1.2 fusion.264
  85.7 1.2 copy.199
  86.9 1.4 fusion.267
  89.4 1.5 fusion.269
  91.0 1.8 copy.200
  92.7 1.4 fusion.270
  94.1 1.2 fusion.271
  96.2 1.4 fusion.273
  100.7 3.5 copy.108
  104.2 45.3 %scatter_custom_fusion = f32[3,768]{0,1:T(8,128)S(1)} fusion(s32[8192]{0:T(1024)} %get-tuple-element.633, f32[8192,3]{1,0:T(8,128)} %bitcast.466, f32[]{:T(128)} %constant.182.clone.1), kind=kCustom, calls=%fused_computation.191 | custom fusion | flops 24576 | bytes 9728 | tf_op jit(solution)/shard_map/scatter-add | solution.py:209
  150.8 22.9 %reduce-scatter.7.cloned.1.call-done = f32[64,9]{1,0:T(8,128)} async-done(((f32[256,9]{1,0:T(8,128)}), f32[64,9]{1,0:T(8,128)}) %reduce-scatter.7.cloned.1.call-update) | async-done | bytes 2320
  176.0 2.7 collective-permute-done.5
  179.3 3.8 %collective-permute-start.9 = (f32[3,1,64]{2,0,1:T(4,128)S(1)}, f32[3,1,64]{2,0,1:T(4,128)S(1)}, u32[]{:S(2)}, u32[]{:S(2)}) collective-permute-start(f32[3,1,64]{2,0,1:T(4,128)S(1)} %bitcast.491), channel_id=1, source_target_pairs={{1,0},{2,1},{3,2},{0,3},{5,4},{6,5},{7,6},{4,7},{9,8},{10,9},{11,1... | collective-permute-start | bytes 2312 | tf_op jit(solution)/shard_map/ppermute | solution.py:162
  183.1 1.6 collective-permute-done.7
  184.7 5.4 %collective-permute-done.8 = f32[3,1,64]{2,0,1:T(4,128)S(1)} collective-permute-done((f32[3,1,64]{2,0,1:T(4,128)S(1)}, f32[3,1,64]{2,0,1:T(4,128)S(1)}, u32[]{:S(2)}, u32[]{:S(2)}) %collective-permute-start.8) | collective-permute-done | bytes 800 | tf_op jit(solution)/shard_map/ppermute | solution.py:160
  192.1 2.6 collective-permute-done.10
  196.4 77.5 %while.27 = (s32[]{:T(128)}, f32[2,32]{1,0:T(2,128)}, f32[2,3,32,128]{3,1,2,0:T(4,128)}, f32[2,32,128]{2,0,1:T(2,128)S(1)}, s32[2,32,128]{2,1,0:T(8,128)}, /*ind...) while((s32[]{:T(128)}, f32[2,32]{1,0:T(2,128)}, ...), condition=%wide.region_10.12_spmd, body=%wide.region_7.11_spmd.sunk | while | flops 271367680 | bytes 45020100 | solution.py:198
  197.2 11.8 %gather_fusion.1 = f32[4096,3]{1,0:T(8,128)S(1)} fusion(f32[3,768]{0,1:T(8,128)} %get-tuple-element.988, s32[4096]{0:T(1024)S(1)} %bitcast_clamp_fusion.5), kind=kCustom, calls=%fused_computation.1.clone.clone.1 | custom fusion | bytes 114688 | tf_op jit(solution)/shard_map/while/body/eval_jaxpr/jit(_take)/gather | solution.py:190
  211.6 2.1 maximum_add_fusion.7
  213.7 1.2 fusion.303
  218.0 1.2 copy.207
  219.2 1.4 fusion.306
  221.7 1.3 dynamic_update_slice.27
  222.9 2.4 fusion.309
  225.3 1.7 copy.208
  227.9 1.6 fusion.312
  229.5 1.3 multiply_bitcast_fusion.7
  230.8 1.4 fusion.313
  233.4 1.1 fusion.315
  235.9 11.8 %gather_fusion.1 = f32[4096,3]{1,0:T(8,128)S(1)} fusion(f32[3,768]{0,1:T(8,128)} %get-tuple-element.988, s32[4096]{0:T(1024)S(1)} %bitcast_clamp_fusion.5), kind=kCustom, calls=%fused_computation.1.clone.clone.1 | custom fusion | bytes 114688 | tf_op jit(solution)/shard_map/while/body/eval_jaxpr/jit(_take)/gather | solution.py:190
  250.3 2.1 maximum_add_fusion.7
  252.4 1.2 fusion.303
  256.7 1.2 copy.207
  258.0 1.4 fusion.306
  260.4 1.3 dynamic_update_slice.27
  261.7 2.4 fusion.309
  264.0 1.7 copy.208
  266.6 1.6 fusion.312
  268.2 1.3 multiply_bitcast_fusion.7
  269.5 1.4 fusion.313
  272.1 1.1 fusion.315
  273.9 3.5 copy.116
  277.4 45.2 %scatter_custom_fusion.1 = f32[3,768]{0,1:T(8,128)S(1)} fusion(s32[8192]{0:T(1024)} %get-tuple-element.633, f32[8192,3]{1,0:T(8,128)} %bitcast.465, f32[]{:T(128)} %constant.182.clone.1), kind=kCustom, calls=%fused_computation.189 | custom fusion | flops 24576 | bytes 9728 | tf_op jit(solution)/shard_map/scatter-add | solution.py:209
  323.8 22.9 %reduce-scatter.9.cloned.1.call-done = f32[64,9]{1,0:T(8,128)} async-done(((f32[256,9]{1,0:T(8,128)}), f32[64,9]{1,0:T(8,128)}) %reduce-scatter.9.cloned.1.call-update) | async-done | bytes 2320
  348.6 1.3 reshape.364
  349.9 1.8 collective-permute-done.12
  (403 shorter events, 57.9 us)
Async XLA Ops:
  7.2 166.5 %reduce-scatter.7.cloned.1.call-start = ((), (), s32[]{:S(2)}) async-start(), calls=%async_computation.2 | async-start | bytes 163840
  7.9 21.4 %copy-start.58 = (f32[3,64]{1,0:T(4,128)}, f32[3,64]{1,0:T(4,128)S(1)}, u32[]{:S(2)}) copy-start(f32[3,64]{1,0:T(4,128)S(1)} %multiply_add_fusion.2) | copy-start | bytes 2308
  7.9 10.5 %collective-permute-start.2 = (f32[3,1,64]{2,0,1:T(4,128)S(1)}, f32[3,1,64]{2,0,1:T(4,128)S(1)}, u32[]{:S(2)}, u32[]{:S(2)}) collective-permute-start(f32[3,1,64]{2,0,1:T(4,128)S(1)} %bitcast.487), channel_id=1, source_target_pairs={{1,0},{2,1},{3,2},{0,3},{5,4},{6,5},{7,6},{4,7},{9,8},{10,9},{11,1... | collective-permute-start | bytes 2312 | tf_op jit(solution)/shard_map/ppermute | solution.py:162
  13.0 5.4 %collective-permute-start = (f32[3,1,64]{2,0,1:T(4,128)S(1)}, f32[3,1,64]{2,0,1:T(4,128)S(1)}, u32[]{:S(2)}, u32[]{:S(2)}) collective-permute-start(f32[3,1,64]{2,0,1:T(4,128)S(1)} %bitcast.488), channel_id=1, source_target_pairs={{0,1},{1,2},{2,3},{3,0},{4,5},{5,6},{6,7},{7,4},{8,9},{9,10},{10,1... | collective-permute-start | bytes 2312 | tf_op jit(solution)/shard_map/ppermute | solution.py:160
  18.4 5.4 %collective-permute-start.1 = (f32[3,1,64]{2,0,1:T(4,128)S(1)}, f32[3,1,64]{2,0,1:T(4,128)S(1)}, u32[]{:S(2)}, u32[]{:S(2)}) collective-permute-start(f32[3,1,64]{2,0,1:T(4,128)S(1)} %collective-permute-done), channel_id=1, source_target_pairs={{0,1},{1,2},{2,3},{3,0},{4,5},{5,6},{6,7},{7,4},{8,9},{9,10},{10,1... | collective-permute-start | bytes 2312 | tf_op jit(solution)/shard_map/ppermute | solution.py:160
  18.4 6.0 %copy-start.64 = (s32[1024]{0:T(1024)}, s32[1024]{0:T(1024)S(1)}, u32[]{:S(2)}) copy-start(s32[1024]{0:T(1024)S(1)} %pad_clamp_fusion) | copy-start | bytes 12292
  24.5 2.1 collective-permute-start.4
  24.5 4.0 %collective-permute-start.3 = (f32[3,1,256]{2,1,0:T(1,128)S(1)}, f32[3,1,256]{2,1,0:T(1,128)S(1)}, u32[]{:S(2)}, u32[]{:S(2)}) collective-permute-start(f32[3,1,256]{2,1,0:T(1,128)S(1)} %reshape.353), channel_id=1, source_target_pairs={{0,4},{4,8},{8,12},{12,16},{16,20},{20,24},{24,28},{28,0},{1,5},{5... | collective-permute-start | bytes 9224 | tf_op jit(solution)/shard_map/ppermute | solution.py:27
  29.3 16.3 %copy-start.14 = (f32[3,768]{0,1:T(8,128)}, f32[3,768]{0,1:T(8,128)S(1)}, u32[]{:S(2)}) copy-start(f32[3,768]{0,1:T(8,128)S(1)} %get-tuple-element.926) | copy-start | bytes 27652 | tf_op jit(solution)/shard_map/while
  29.3 16.3 %copy-start.36 = (f32[2,32,128]{2,0,1:T(2,128)}, f32[2,32,128]{2,0,1:T(2,128)S(1)}, u32[]{:S(2)}) copy-start(f32[2,32,128]{2,0,1:T(2,128)S(1)} %get-tuple-element.924) | copy-start | bytes 98308 | tf_op jit(solution)/shard_map/while
  29.3 16.3 %copy-start.40 = (f32[2,32,128]{2,0,1:T(2,128)}, f32[2,32,128]{2,0,1:T(2,128)S(1)}, u32[]{:S(2)}) copy-start(f32[2,32,128]{2,0,1:T(2,128)S(1)} %get-tuple-element.928) | copy-start | bytes 98308 | tf_op jit(solution)/shard_map/while
  29.3 16.3 %copy-start.56 = (f32[2,3,32]{2,1,0:T(4,128)}, f32[2,3,32]{2,1,0:T(4,128)S(1)}, u32[]{:S(2)}) copy-start(f32[2,3,32]{2,1,0:T(4,128)S(1)} %get-tuple-element.927) | copy-start | bytes 2308 | tf_op jit(solution)/shard_map/while
  29.3 14.2 %copy-start.34 = (bf16[32,64]{1,0:T(8,128)(2,1)S(1)}, bf16[32,64]{1,0:T(8,128)(2,1)}, u32[]{:S(2)}) copy-start(bf16[32,64]{1,0:T(8,128)(2,1)} %get-tuple-element.931) | copy-start | bytes 12292 | tf_op jit(solution)/shard_map/while
  42.5 4.6 %copy-start.18 = (f32[1,32,128]{2,0,1:T(1,128)}, f32[1,32,128]{2,0,1:T(1,128)S(1)}, u32[]{:S(2)}) copy-start(f32[1,32,128]{2,0,1:T(1,128)S(1)} %get-tuple-element.854) | copy-start | bytes 49156 | tf_op jit(solution)/shard_map/while
  42.6 4.6 %copy-start.12 = (f32[2,32,128]{2,0,1:T(2,128)}, f32[2,32,128]{2,0,1:T(2,128)S(1)}, u32[]{:S(2)}) copy-start(f32[2,32,128]{2,0,1:T(2,128)S(1)} %slice.247) | copy-start | bytes 98308 | tf_op jit(solution)/shard_map/while
  47.1 5.6 %copy-start.7 = (bf16[240,240]{1,0:T(8,128)(2,1)S(1)}, bf16[240,240]{1,0:T(8,128)(2,1)}, u32[]{:S(2)}) copy-start(bf16[240,240]{1,0:T(8,128)(2,1)} %get-tuple-element.938) | copy-start | bytes 345604 | tf_op jit(solution)/shard_map/while
  47.1 5.6 %copy-start.50 = (f32[240]{0:T(256)S(1)}, f32[240]{0:T(256)}, u32[]{:S(2)}) copy-start(f32[240]{0:T(256)} %get-tuple-element.939) | copy-start | bytes 2884 | tf_op jit(solution)/shard_map/while
  49.3 4.4 %copy-start.9 = (f32[32,4,128]{2,1,0:T(4,128)}, f32[32,4,128]{2,1,0:T(4,128)S(1)}, u32[]{:S(2)}) copy-start(f32[32,4,128]{2,1,0:T(4,128)S(1)} %convolution_multiply_fusion.6) | copy-start | bytes 196612 | tf_op jit(solution)/shard_map/while
  55.3 4.7 %copy-start.22 = (bf16[3,32,128]{2,0,1:T(4,128)(2,1)S(1)}, bf16[3,32,128]{2,0,1:T(4,128)(2,1)}, u32[]{:S(2)}) copy-start(bf16[3,32,128]{2,0,1:T(4,128)(2,1)} %copy-done.21) | copy-start | bytes 73732 | tf_op jit(solution)/shard_map/while
  55.3 4.7 %copy-start.33 = (bf16[1,32,128]{2,0,1:T(2,128)(2,1)S(1)}, bf16[1,32,128]{2,0,1:T(2,128)(2,1)}, u32[]{:S(2)}) copy-start(bf16[1,32,128]{2,0,1:T(2,128)(2,1)} %copy-done.32) | copy-start | bytes 24580 | tf_op jit(solution)/shard_map/while
  65.0 16.3 %copy-start.14 = (f32[3,768]{0,1:T(8,128)}, f32[3,768]{0,1:T(8,128)S(1)}, u32[]{:S(2)}) copy-start(f32[3,768]{0,1:T(8,128)S(1)} %get-tuple-element.926) | copy-start | bytes 27652 | tf_op jit(solution)/shard_map/while
  65.0 16.3 %copy-start.36 = (f32[2,32,128]{2,0,1:T(2,128)}, f32[2,32,128]{2,0,1:T(2,128)S(1)}, u32[]{:S(2)}) copy-start(f32[2,32,128]{2,0,1:T(2,128)S(1)} %get-tuple-element.924) | copy-start | bytes 98308 | tf_op jit(solution)/shard_map/while
  65.0 16.3 %copy-start.40 = (f32[2,32,128]{2,0,1:T(2,128)}, f32[2,32,128]{2,0,1:T(2,128)S(1)}, u32[]{:S(2)}) copy-start(f32[2,32,128]{2,0,1:T(2,128)S(1)} %get-tuple-element.928) | copy-start | bytes 98308 | tf_op jit(solution)/shard_map/while
  65.0 16.3 %copy-start.56 = (f32[2,3,32]{2,1,0:T(4,128)}, f32[2,3,32]{2,1,0:T(4,128)S(1)}, u32[]{:S(2)}) copy-start(f32[2,3,32]{2,1,0:T(4,128)S(1)} %get-tuple-element.927) | copy-start | bytes 2308 | tf_op jit(solution)/shard_map/while
  65.1 14.2 %copy-start.34 = (bf16[32,64]{1,0:T(8,128)(2,1)S(1)}, bf16[32,64]{1,0:T(8,128)(2,1)}, u32[]{:S(2)}) copy-start(bf16[32,64]{1,0:T(8,128)(2,1)} %get-tuple-element.931) | copy-start | bytes 12292 | tf_op jit(solution)/shard_map/while
  78.2 4.6 %copy-start.18 = (f32[1,32,128]{2,0,1:T(1,128)}, f32[1,32,128]{2,0,1:T(1,128)S(1)}, u32[]{:S(2)}) copy-start(f32[1,32,128]{2,0,1:T(1,128)S(1)} %get-tuple-element.854) | copy-start | bytes 49156 | tf_op jit(solution)/shard_map/while
  78.3 4.6 %copy-start.12 = (f32[2,32,128]{2,0,1:T(2,128)}, f32[2,32,128]{2,0,1:T(2,128)S(1)}, u32[]{:S(2)}) copy-start(f32[2,32,128]{2,0,1:T(2,128)S(1)} %slice.247) | copy-start | bytes 98308 | tf_op jit(solution)/shard_map/while
  82.8 5.6 %copy-start.7 = (bf16[240,240]{1,0:T(8,128)(2,1)S(1)}, bf16[240,240]{1,0:T(8,128)(2,1)}, u32[]{:S(2)}) copy-start(bf16[240,240]{1,0:T(8,128)(2,1)} %get-tuple-element.938) | copy-start | bytes 345604 | tf_op jit(solution)/shard_map/while
  82.8 5.6 %copy-start.50 = (f32[240]{0:T(256)S(1)}, f32[240]{0:T(256)}, u32[]{:S(2)}) copy-start(f32[240]{0:T(256)} %get-tuple-element.939) | copy-start | bytes 2884 | tf_op jit(solution)/shard_map/while
  85.0 4.4 %copy-start.9 = (f32[32,4,128]{2,1,0:T(4,128)}, f32[32,4,128]{2,1,0:T(4,128)S(1)}, u32[]{:S(2)}) copy-start(f32[32,4,128]{2,1,0:T(4,128)S(1)} %convolution_multiply_fusion.6) | copy-start | bytes 196612 | tf_op jit(solution)/shard_map/while
  91.0 4.7 %copy-start.22 = (bf16[3,32,128]{2,0,1:T(4,128)(2,1)S(1)}, bf16[3,32,128]{2,0,1:T(4,128)(2,1)}, u32[]{:S(2)}) copy-start(bf16[3,32,128]{2,0,1:T(4,128)(2,1)} %copy-done.21) | copy-start | bytes 73732 | tf_op jit(solution)/shard_map/while
  91.0 4.7 %copy-start.33 = (bf16[1,32,128]{2,0,1:T(2,128)(2,1)S(1)}, bf16[1,32,128]{2,0,1:T(2,128)(2,1)}, u32[]{:S(2)}) copy-start(bf16[1,32,128]{2,0,1:T(2,128)(2,1)} %copy-done.32) | copy-start | bytes 24580 | tf_op jit(solution)/shard_map/while
  104.2 71.1 %copy-start.49 = (f32[2,3,32,128]{3,1,2,0:T(4,128)S(1)}, f32[2,3,32,128]{3,1,2,0:T(4,128)}, u32[]{:S(2)}) copy-start(f32[2,3,32,128]{3,1,2,0:T(4,128)} %get-tuple-element.460) | copy-start | bytes 294916
  104.2 74.5 %copy-start.59 = (f32[3,64]{1,0:T(4,128)S(1)}, f32[3,64]{1,0:T(4,128)}, u32[]{:S(2)}) copy-start(f32[3,64]{1,0:T(4,128)} %copy-done.58) | copy-start | bytes 2308
  104.2 74.5 %copy-start.62 = (f32[3,64]{1,0:T(4,128)S(1)}, f32[3,64]{1,0:T(4,128)}, u32[]{:S(2)}) copy-start(f32[3,64]{1,0:T(4,128)} %param.22) | copy-start | bytes 2308
  104.2 74.5 %copy-start.63 = (f32[3,64]{1,0:T(4,128)S(1)}, f32[3,64]{1,0:T(4,128)}, u32[]{:S(2)}) copy-start(f32[3,64]{1,0:T(4,128)} %param.23) | copy-start | bytes 2308
  104.2 92.2 %copy-start.1 = (bf16[2048,240]{0,1:T(8,128)(2,1)S(1)}, bf16[2048,240]{0,1:T(8,128)(2,1)}, u32[]{:S(2)}) copy-start(bf16[2048,240]{0,1:T(8,128)(2,1)} %get-tuple-element.1006) | copy-start | bytes 2949124
  104.2 92.2 %copy-start.8 = (bf16[240,240]{1,0:T(8,128)(2,1)S(1)}, bf16[240,240]{1,0:T(8,128)(2,1)}, u32[]{:S(2)}) copy-start(bf16[240,240]{1,0:T(8,128)(2,1)} %get-tuple-element.1007) | copy-start | bytes 345604
  104.2 92.2 %copy-start.35 = (bf16[32,64]{1,0:T(8,128)(2,1)S(1)}, bf16[32,64]{1,0:T(8,128)(2,1)}, u32[]{:S(2)}) copy-start(bf16[32,64]{1,0:T(8,128)(2,1)} %get-tuple-element.1008) | copy-start | bytes 12292
  150.7 196.0 %reduce-scatter.9.cloned.1.call-start = ((), (), s32[]{:S(2)}) async-start(), calls=%async_computation.3 | async-start | bytes 163840
  174.7 1.3 collective-permute-start.6
  174.8 3.9 %collective-permute-start.5 = (f32[3,1,64]{2,0,1:T(4,128)S(1)}, f32[3,1,64]{2,0,1:T(4,128)S(1)}, u32[]{:S(2)}, u32[]{:S(2)}) collective-permute-start(f32[3,1,64]{2,0,1:T(4,128)S(1)} %copy.135), channel_id=1, source_target_pairs={{0,4},{4,8},{8,12},{12,16},{16,20},{20,24},{24,28},{28,0},{1,5},{5... | collective-permute-start | bytes 2312 | tf_op jit(solution)/shard_map/ppermute | solution.py:27
  179.3 17.2 %copy-start.60 = (f32[3,64]{1,0:T(4,128)}, f32[3,64]{1,0:T(4,128)S(1)}, u32[]{:S(2)}) copy-start(f32[3,64]{1,0:T(4,128)S(1)} %get-tuple-element.613) | copy-start | bytes 2308
  179.3 5.4 %collective-permute-start.7 = (f32[3,1,64]{2,0,1:T(4,128)S(1)}, f32[3,1,64]{2,0,1:T(4,128)S(1)}, u32[]{:S(2)}, u32[]{:S(2)}) collective-permute-start(f32[3,1,64]{2,0,1:T(4,128)S(1)} %bitcast.490), channel_id=1, source_target_pairs={{0,1},{1,2},{2,3},{3,0},{4,5},{5,6},{6,7},{7,4},{8,9},{9,10},{10,1... | collective-permute-start | bytes 2312 | tf_op jit(solution)/shard_map/ppermute | solution.py:160
  179.3 5.4 %collective-permute-start.9 = (f32[3,1,64]{2,0,1:T(4,128)S(1)}, f32[3,1,64]{2,0,1:T(4,128)S(1)}, u32[]{:S(2)}, u32[]{:S(2)}) collective-permute-start(f32[3,1,64]{2,0,1:T(4,128)S(1)} %bitcast.491), channel_id=1, source_target_pairs={{1,0},{2,1},{3,2},{0,3},{5,4},{6,5},{7,6},{4,7},{9,8},{10,9},{11,1... | collective-permute-start | bytes 2312 | tf_op jit(solution)/shard_map/ppermute | solution.py:162
  184.7 5.4 %collective-permute-start.8 = (f32[3,1,64]{2,0,1:T(4,128)S(1)}, f32[3,1,64]{2,0,1:T(4,128)S(1)}, u32[]{:S(2)}, u32[]{:S(2)}) collective-permute-start(f32[3,1,64]{2,0,1:T(4,128)S(1)} %collective-permute-done.7), channel_id=1, source_target_pairs={{0,1},{1,2},{2,3},{3,0},{4,5},{5,6},{6,7},{7,4},{8,9},{9,10},{10,1... | collective-permute-start | bytes 2312 | tf_op jit(solution)/shard_map/ppermute | solution.py:160
  190.8 1.3 collective-permute-start.11
  190.8 4.0 %collective-permute-start.10 = (f32[3,1,256]{2,1,0:T(1,128)S(1)}, f32[3,1,256]{2,1,0:T(1,128)S(1)}, u32[]{:S(2)}, u32[]{:S(2)}) collective-permute-start(f32[3,1,256]{2,1,0:T(1,128)S(1)} %reshape.359), channel_id=1, source_target_pairs={{0,4},{4,8},{8,12},{12,16},{16,20},{20,24},{24,28},{28,0},{1,5},{5... | collective-permute-start | bytes 9224 | tf_op jit(solution)/shard_map/ppermute | solution.py:27
  196.4 13.3 %copy-start.54 = (f32[2,3,32]{2,1,0:T(4,128)}, f32[2,3,32]{2,1,0:T(4,128)S(1)}, u32[]{:S(2)}) copy-start(f32[2,3,32]{2,1,0:T(4,128)S(1)} %get-tuple-element.989) | copy-start | bytes 2308 | tf_op jit(solution)/shard_map/while
  196.5 17.2 %copy-start.38 = (f32[2,32,128]{2,0,1:T(2,128)}, f32[2,32,128]{2,0,1:T(2,128)S(1)}, u32[]{:S(2)}) copy-start(f32[2,32,128]{2,0,1:T(2,128)S(1)} %get-tuple-element.986) | copy-start | bytes 98308 | tf_op jit(solution)/shard_map/while
  196.5 17.2 %copy-start.42 = (f32[2,32,128]{2,0,1:T(2,128)}, f32[2,32,128]{2,0,1:T(2,128)S(1)}, u32[]{:S(2)}) copy-start(f32[2,32,128]{2,0,1:T(2,128)S(1)} %get-tuple-element.990) | copy-start | bytes 98308 | tf_op jit(solution)/shard_map/while
  210.6 4.6 %copy-start.16 = (f32[1,32,128]{2,0,1:T(1,128)}, f32[1,32,128]{2,0,1:T(1,128)S(1)}, u32[]{:S(2)}) copy-start(f32[1,32,128]{2,0,1:T(1,128)S(1)} %get-tuple-element.879) | copy-start | bytes 49156 | tf_op jit(solution)/shard_map/while
  210.6 4.5 %copy-start.10 = (f32[2,32,128]{2,0,1:T(2,128)}, f32[2,32,128]{2,0,1:T(2,128)S(1)}, u32[]{:S(2)}) copy-start(f32[2,32,128]{2,0,1:T(2,128)S(1)} %slice.259) | copy-start | bytes 98308 | tf_op jit(solution)/shard_map/while
  215.1 5.6 %copy-start.51 = (f32[240]{0:T(256)S(1)}, f32[240]{0:T(256)}, u32[]{:S(2)}) copy-start(f32[240]{0:T(256)} %get-tuple-element.1000) | copy-start | bytes 2884 | tf_op jit(solution)/shard_map/while
  235.2 13.2 %copy-start.54 = (f32[2,3,32]{2,1,0:T(4,128)}, f32[2,3,32]{2,1,0:T(4,128)S(1)}, u32[]{:S(2)}) copy-start(f32[2,3,32]{2,1,0:T(4,128)S(1)} %get-tuple-element.989) | copy-start | bytes 2308 | tf_op jit(solution)/shard_map/while
  235.2 17.2 %copy-start.38 = (f32[2,32,128]{2,0,1:T(2,128)}, f32[2,32,128]{2,0,1:T(2,128)S(1)}, u32[]{:S(2)}) copy-start(f32[2,32,128]{2,0,1:T(2,128)S(1)} %get-tuple-element.986) | copy-start | bytes 98308 | tf_op jit(solution)/shard_map/while
  235.2 17.2 %copy-start.42 = (f32[2,32,128]{2,0,1:T(2,128)}, f32[2,32,128]{2,0,1:T(2,128)S(1)}, u32[]{:S(2)}) copy-start(f32[2,32,128]{2,0,1:T(2,128)S(1)} %get-tuple-element.990) | copy-start | bytes 98308 | tf_op jit(solution)/shard_map/while
  249.3 4.6 %copy-start.16 = (f32[1,32,128]{2,0,1:T(1,128)}, f32[1,32,128]{2,0,1:T(1,128)S(1)}, u32[]{:S(2)}) copy-start(f32[1,32,128]{2,0,1:T(1,128)S(1)} %get-tuple-element.879) | copy-start | bytes 49156 | tf_op jit(solution)/shard_map/while
  249.4 4.5 %copy-start.10 = (f32[2,32,128]{2,0,1:T(2,128)}, f32[2,32,128]{2,0,1:T(2,128)S(1)}, u32[]{:S(2)}) copy-start(f32[2,32,128]{2,0,1:T(2,128)S(1)} %slice.259) | copy-start | bytes 98308 | tf_op jit(solution)/shard_map/while
  253.8 5.6 %copy-start.51 = (f32[240]{0:T(256)S(1)}, f32[240]{0:T(256)}, u32[]{:S(2)}) copy-start(f32[240]{0:T(256)} %get-tuple-element.1000) | copy-start | bytes 2884 | tf_op jit(solution)/shard_map/while
  277.4 70.9 %copy-start.46 = (f32[2,3,32,128]{3,1,2,0:T(4,128)S(1)}, f32[2,3,32,128]{3,1,2,0:T(4,128)}, u32[]{:S(2)}) copy-start(f32[2,3,32,128]{3,1,2,0:T(4,128)} %get-tuple-element.461) | copy-start | bytes 294916
  277.4 74.3 %copy-start.61 = (f32[3,64]{1,0:T(4,128)S(1)}, f32[3,64]{1,0:T(4,128)}, u32[]{:S(2)}) copy-start(f32[3,64]{1,0:T(4,128)} %get-tuple-element.614) | copy-start | bytes 2308
  347.7 2.2 collective-permute-start.13
  347.8 3.9 %collective-permute-start.12 = (f32[3,1,64]{2,0,1:T(4,128)S(1)}, f32[3,1,64]{2,0,1:T(4,128)S(1)}, u32[]{:S(2)}, u32[]{:S(2)}) collective-permute-start(f32[3,1,64]{2,0,1:T(4,128)S(1)} %copy.138), channel_id=1, source_target_pairs={{0,4},{4,8},{8,12},{12,16},{16,20},{20,24},{24,28},{28,0},{1,5},{5... | collective-permute-start | bytes 2312 | tf_op jit(solution)/shard_map/ppermute | solution.py:27
  (70 other events, 142.3 us)
Sparse Core Ops, SparseCore 0:
  150.8 22.7 reduce-scatter.6
  323.9 22.7 reduce-scatter.8
